TPU v7x, 32 devices: a whole 2x2x4 slice. The times are simulated.
32 devices in a mesh: dp: 8 (over z, x), row: 2 (over y), col: 2 (over core).
Axes of the slice: x: 2, y: 2, z: 4, core: 2. Of those that a mesh axis runs over, the one named last changes fastest.
Arguments:
- block_input: bfloat16 [6272, 512], P('dp', 'row'), may hold values from -6 to 6
- out_grad: bfloat16 [6272, 512], P('dp', 'row'), may hold values from -6 to 6
- first_gain: float32 [512], P('row'), may hold values from 0.5 to 1.5
- first_shift: float32 [512], P('row'), may hold values from -3 to 3
- qkv_weight: bfloat16 [512, 3, 512], P('row', None, 'col'), may hold values from -0.25 to 0.25
- query_bias: float32 [512], P('col'), may hold values from -3 to 3
- value_bias: float32 [512], P('col'), may hold values from -0.6 to 0.6
- position_table: float32 [169, 16], P(None, 'col'), may hold values from -6 to 306
- position_index: int32 [49, 49], replicated, may hold values from 0 to 168
- proj_weight: bfloat16 [512, 512], P('col', 'row'), may hold values from -2 to 2
- proj_bias: float32 [512], P('row'), may hold values from -1.2 to 1.2
- second_gain: float32 [512], P('row'), may hold values from 0.5 to 1.5
- second_shift: float32 [512], P('row'), may hold values from -3 to 3
- expand_weight: bfloat16 [512, 2048], P('row', 'col'), may hold values from -0.5 to 0.5
- expand_bias: float32 [2048], P('col'), may hold values from -3 to 3
- reduce_weight: bfloat16 [2048, 512], P('col', 'row'), may hold values from -0.5 to 0.5
- reduce_bias: float32 [512], P('row'), may hold values from -3 to 3
Outputs:
- block_output: bfloat16 [6272, 512], P('dp', 'row')
- input_grad: float32 [6272, 512], P('dp', 'row')
- first_gain_grad: float32 [512], P('row')
- first_shift_grad: float32 [512], P('row')
- qkv_weight_grad: float32 [512, 3, 512], P('row', None, 'col')
- query_bias_grad: float32 [512], P('col')
- value_bias_grad: float32 [512], P('col')
- position_table_grad: float32 [169, 16], P(None, 'col')
- proj_weight_grad: float32 [512, 512], P('col', 'row')
- proj_bias_grad: float32 [512], P('row')
- second_gain_grad: float32 [512], P('row')
- second_shift_grad: float32 [512], P('row')
- expand_weight_grad: float32 [512, 2048], P('row', 'col')
- expand_bias_grad: float32 [2048], P('col')
- reduce_weight_grad: float32 [2048, 512], P('col', 'row')
- reduce_bias_grad: float32 [512], P('row')
Inputs may be any that keep to these rules, and one draw needn't show every extreme that they name: `position_index`: entries name rows of position_table.
All inputs are finite; a program needn't handle non-finite values.
Results may differ from a plain program's by a relative error of at most 0.012.
The roundings to bfloat16 on the way count: a program that leaves them out, or rounds other values in their place, can miss the bound.
Values may be sent and summed in bfloat16 or wider, within the bound.
A program may use at most 64 MiB of HBM per device.

v0:
```python
import functools
from types import SimpleNamespace

import jax
import jax.numpy as jnp
from jax import lax
from jax.experimental import pallas as pl
from jax.experimental.pallas import tpu as pltpu
from jax.sharding import PartitionSpec as P

EPSILON = 1e-05
ROOT_HALF = 0.7071067811865476
GAUSS_PEAK = 0.3989422804014327
SIDE = 7
WINDOW = SIDE * SIDE
IMAGE = 4 * WINDOW
TOK = 208
PAD = 64
ROWS = 4 * PAD
F32 = jnp.float32
BF16 = jnp.bfloat16
VMEM = pl.BlockSpec(memory_space=pltpu.VMEM)
MESH = pl.DeviceIdType.MESH
LIMIT = 60 * 1024 * 1024


def dot(left, right):
    return jnp.dot(left, right, preferred_element_type=F32)


def dot_t(left, right):
    return lax.dot_general(left, right, (((1,), (1,)), ((), ())), preferred_element_type=F32)


def t_dot(left, right):
    return lax.dot_general(left, right, (((0,), (0,)), ((), ())), preferred_element_type=F32)


def thirds(values):
    high = values.astype(BF16)
    rest = values - high.astype(F32)
    middle = rest.astype(BF16)
    return high, middle, (rest - middle.astype(F32)).astype(BF16)


def norm(values):
    center = jnp.mean(values, axis=-1, keepdims=True)
    shifted = values - center
    spread = jnp.mean(shifted * shifted, axis=-1, keepdims=True)
    inverse = lax.rsqrt(spread + EPSILON)
    return shifted * inverse, inverse


def norm_backward(upstream, gain, normed, inverse):
    scaled = upstream * gain
    return inverse * (
        scaled
        - jnp.mean(scaled, axis=-1, keepdims=True)
        - normed * jnp.mean(scaled * normed, axis=-1, keepdims=True)
    )


def head_mask(heads, width):
    size = width // heads
    head = lax.broadcasted_iota(jnp.int32, (heads, 1, width), 0)
    lane = lax.broadcasted_iota(jnp.int32, (heads, 1, width), 2)
    return (lane >= head * size) & (lane < (head + 1) * size)


def stack_heads(rows, mask):
    heads = mask.shape[0]
    wide = jnp.where(mask, rows.astype(F32)[None], 0.0)
    return wide.reshape(heads * rows.shape[0], rows.shape[1]).astype(BF16)


def fold_heads(stacked, mask):
    heads = mask.shape[0]
    split = stacked.reshape(heads, stacked.shape[0] // heads, stacked.shape[1])
    return jnp.sum(jnp.where(mask, split, 0.0), axis=0)


def softmax(scores):
    top = jnp.max(scores, axis=-1, keepdims=True)
    powers = jnp.exp(scores - top)
    return powers / jnp.sum(powers, axis=-1, keepdims=True)


def block_kernel(n, size, names, *refs):
    r = SimpleNamespace(**dict(zip(names, refs)))
    me = lax.axis_index("dp")
    row, col = lax.axis_index("row"), lax.axis_index("col")
    cores = lax.axis_size("col")
    parity, place = lax.rem(me, 2), me // 2
    peers = n // 2
    over_col, over_row = {"col": 1 - col}, {"row": 1 - row}
    pair = {"dp": me + 1 - 2 * parity}
    half, width, hid = r.x_in.shape[1], r.wp.shape[0], r.we.shape[1]
    heads = r.table.shape[1]
    scale = (width // heads) ** (-0.5)
    images = r.x_in.shape[0] // IMAGE
    slices = hid // half
    full = 2 * half
    mine = row * cores + col
    theirs = (1 - row) * cores + col
    wide, block = size // 2, size // n
    chunks = r.o_f.shape[0] // size
    live = {}

    def peer_of(k):
        there = lax.rem(place + k, peers)
        return there, {"dp": 2 * there + parity}

    barrier = pltpu.get_barrier_semaphore()
    for device in [over_col, over_row, pair] + [peer_of(k)[1] for k in range(1, peers)]:
        pl.semaphore_signal(barrier, inc=1, device_id=device, device_id_type=MESH)

    def start(key, src, dst, device):
        index = len(live)
        live[key] = pltpu.make_async_remote_copy(
            src, dst, r.sems.at[0, index], r.sems.at[1, index], device, MESH
        )
        live[key].start()

    def arrived(*key):
        live[key].wait_recv()

    def tokens_of(image):
        return pl.ds(pl.multiple_of(image * TOK, 16), TOK)

    spot = lax.broadcasted_iota(jnp.int32, (TOK, images * IMAGE), 1)
    line = lax.broadcasted_iota(jnp.int32, (TOK, images * IMAGE), 0)
    line = jnp.where(line < IMAGE, line, -IMAGE * images)
    for k in range(images):
        r.sel[k * TOK:(k + 1) * TOK] = jnp.where(spot == line + k * IMAGE, 1.0, 0.0).astype(BF16)
    place_in = lax.broadcasted_iota(jnp.int32, (ROWS, TOK), 0)
    spot = lax.broadcasted_iota(jnp.int32, (ROWS, TOK), 1)
    window, i = place_in >> 6, place_in & (PAD - 1)
    i_row = (i * 37) >> 8
    target = ((window >> 1) * SIDE + i_row) * (2 * SIDE) + (window & 1) * SIDE + i - SIDE * i_row
    target = jnp.where(i < WINDOW, target, -1)
    r.perm[...] = jnp.where(spot == target, 1.0, 0.0).astype(BF16)
    sel_mine, sel_theirs = r.sel[tokens_of(mine)], r.sel[tokens_of(theirs)]
    r.x_away[...] = dot(sel_theirs, r.x_in[...]).astype(BF16)
    r.g_away[...] = dot(sel_theirs, r.g_in[...]).astype(BF16)
    r.vec_own[...] = jnp.zeros_like(r.vec_own)
    r.cvec_own[...] = jnp.zeros_like(r.cvec_own)
    for k, ref in enumerate((r.gain1, r.shift1, r.bias_p, r.gain2, r.shift2, r.bias_r)):
        r.vec_own[k:k + 1] = ref[...]
    r.cvec_own[0:1] = r.bias_q[...]
    r.cvec_own[1:2] = r.bias_v[...]
    for k in range(slices):
        r.cvec_own[2 + k:3 + k] = r.bias_e[:, k * half:(k + 1) * half]
    pl.semaphore_wait(barrier, peers + 2)

    weights = {
        "q": (r.wq, r.q_xo, r.q_ox, r.q_xx, 2),
        "p": (r.wp, r.p_xo, r.p_ox, r.p_xx, 1),
        "e": (r.we, r.e_xo, r.e_ox, r.e_xx, 2),
        "r": (r.wr, r.r_xo, r.r_ox, r.r_xx, 2),
    }

    def pieces(name, side):
        rows, count = weights[name][0].shape[0], weights[name][4]
        step = rows // (2 * count)
        for p in range(count):
            yield p, pl.ds(pl.multiple_of(side * (rows // 2) + p * step, step), step)

    def fetch(name):
        oo, xo, ox, _, _ = weights[name]
        for p, rows in pieces(name, parity):
            start((name, "y", p), oo.at[rows], xo.at[rows], over_row)
        start((name, "c"), oo, ox, over_col)

    def relay(name):
        _, xo, _, xx, _ = weights[name]
        for p, rows in pieces(name, parity):
            arrived(name, "y", p)
            start((name, "x", p), xo.at[rows], xo.at[rows], pair)
            start((name, "cy", p), xo.at[rows], xx.at[rows], over_col)

    def relay_back(name):
        _, xo, _, xx, _ = weights[name]
        for p, rows in pieces(name, 1 - parity):
            arrived(name, "x", p)
            start((name, "cx", p), xo.at[rows], xx.at[rows], over_col)

    def ready(name):
        arrived(name, "c")
        for p in range(weights[name][4]):
            arrived(name, "cy", p)
            arrived(name, "cx", p)

    start(("x",), r.x_away, r.x_oth, over_row)
    start(("vec",), r.vec_own, r.vec_oth, over_row)
    start(("cvec",), r.cvec_own, r.cvec_oth, over_col)
    fetch("q")
    fetch("p")
    fetch("e")
    start(("g",), r.g_away, r.g_oth, over_row)
    fetch("r")

    entries = r.table.shape[0]
    which = lax.broadcasted_iota(jnp.int32, (entries, WINDOW * PAD), 0)
    r.hot[...] = jnp.where(which == r.index[...], 1.0, 0.0).astype(BF16)
    spread = sum(t_dot(part, r.hot[...]) for part in thirds(r.table[...]))
    lane = lax.broadcasted_iota(jnp.int32, (heads, PAD), 1)
    r.b_own[...] = jnp.zeros_like(r.b_own)
    for k in range(WINDOW):
        r.b_own[pl.ds(k, heads, stride=PAD), :] = jnp.where(
            lane < WINDOW, spread[:, k * PAD:(k + 1) * PAD], -1e30
        )
    start(("bias",), r.b_own, r.b_oth, over_col)
    x_own = dot(sel_mine, r.x_in[...]).astype(BF16)
    grad_own = dot(sel_mine, r.g_in[...]).astype(BF16)
    mask = head_mask(heads, width)

    arrived("x")
    arrived("vec")
    rvec = jnp.concatenate([r.vec_own[...], r.vec_oth[...]], axis=1)
    x = dot(r.perm[...], jnp.concatenate([x_own, r.x_oth[...]], axis=1))
    normed, inverse_one = norm(x)
    r.n_one[...] = normed
    r.ln_one[...] = (normed * rvec[0:1] + rvec[1:2]).astype(BF16)
    relay("q")
    relay_back("q")
    relay("p")
    arrived("cvec")
    q_side = (r.wq, r.q_ox), (r.q_xo, r.q_xx)
    p_side = (r.wp, r.p_ox), (r.p_xo, r.p_xx)
    e_side = (r.we, r.e_ox), (r.e_xo, r.e_xx)
    r_side = (r.wr, r.r_ox), (r.r_xo, r.r_xx)
    bias_refs = (r.b_own, r.b_oth)
    cvecs = (r.cvec_own, r.cvec_oth)
    step_of = {(0, 1): ("relay_back", "p"), (0, 3): ("relay", "e"), (1, 1): ("relay_back", "e"), (1, 2): ("relay", "r")}
    for b in range(2):
        cols = slice(b * width, (b + 1) * width)
        if b == 1:
            ready("q")
            arrived("bias")
        for s, out in enumerate((r.q, r.k, r.v)):
            part = slice(s * width, (s + 1) * width)
            linear = dot(r.ln_one[:, :half], q_side[0][b][:, part]) + dot(
                r.ln_one[:, half:], q_side[1][b][:, part]
            )
            if s == 0:
                linear = (linear + cvecs[b][0:1]) * scale
            if s == 2:
                linear = linear + cvecs[b][1:2]
            out[:, cols] = linear.astype(BF16)
        for w in range(4):
            rows = slice(w * PAD, (w + 1) * PAD)
            scores = dot_t(stack_heads(r.q[rows, cols], mask), r.k[rows, cols]) + bias_refs[b][...]
            probs = softmax(scores)
            r.probs[b * 4 + w] = probs
            r.mixed[rows, cols] = fold_heads(dot(probs.astype(BF16), r.v[rows, cols]), mask).astype(BF16)
            if (b, w) in step_of:
                what, name = step_of[b, w]
                (relay if what == "relay" else relay_back)(name)
    ready("p")
    parts = [
        dot(r.mixed[:, :width], p_side[a][0][...]) + dot(r.mixed[:, width:], p_side[a][1][...])
        for a in range(2)
    ]
    middle = x + jnp.concatenate(parts, axis=1) + rvec[2:3]
    r.middle[...] = middle
    normed_two, inverse_two = norm(middle)
    r.ln_two[...] = (normed_two * rvec[3:4] + rvec[4:5]).astype(BF16)
    relay_back("r")
    arrived("g")
    grad = dot(r.perm[...], jnp.concatenate([grad_own, r.g_oth[...]], axis=1))
    r.grad[...] = grad.astype(BF16)
    ready("e")
    ready("r")

    def rows_of(c):
        return slice(c * size, (c + 1) * size)

    begun, rowed = [0], [0]

    def away_done(blocks):
        while (begun[0] + 1) * size <= blocks * half:
            c = begun[0]
            start(("y", c), r.y_b.at[rows_of(c)], r.yr.at[rows_of(c)], over_col)
            start(("z", c), r.z_b.at[rows_of(c)], r.zr.at[rows_of(c)], over_col)
            begun[0] += 1

    def home_done(blocks):
        while (rowed[0] + 1) * size <= blocks * half:
            c = rowed[0]
            rows = rows_of(c)
            arrived("z", c)
            r.xb[rows] = (r.x_f[rows] + r.zr[rows].astype(F32)).astype(BF16)
            start(("r", c), r.xb.at[rows], r.xr.at[rows], over_row)
            rowed[0] += 1

    def stage_pair(c):
        arrived("y", c)
        arrived("r", c)
        rows = rows_of(c)
        r.sf[...] = r.o_f[rows] + r.yr[rows].astype(F32) + r.xr[rows].astype(F32)
        r.sb[rows] = r.sf[...].astype(BF16)
        r.tf[c] = r.sf[pl.ds(pl.multiple_of(parity * wide, wide), wide)]
        away = pl.ds(pl.multiple_of(c * size + (1 - parity) * wide, wide), wide)
        start(("p", c), r.sb.at[away], r.pr.at[c], pair)

    def stage_rest(c):
        arrived("p", c)
        r.tf[c] = r.tf[c] + r.pr[c].astype(F32)
        r.tb[c] = r.tf[c].astype(BF16)
        for k in range(1, peers):
            there, device = peer_of(k)
            piece = pl.ds(pl.multiple_of(there * block, block), block)
            start(("q", c, k), r.tb.at[c, piece], r.qr.at[c, k], device)

    def stage_sum(c):
        total = r.tf[c, pl.ds(pl.multiple_of(place * block, block), block)]
        for k in range(1, peers):
            arrived("q", c, k)
            total = total + r.qr[c, k].astype(F32)
        own = pl.ds(pl.multiple_of(c * size + parity * wide + place * block, block), block)
        r.gb[own] = total.astype(BF16)
        for k in range(1, peers):
            start(("g", c, k), r.gb.at[own], r.gb.at[own], peer_of(k)[1])

    def stage_back(c):
        for k in range(1, peers):
            arrived("g", c, k)
        part = pl.ds(pl.multiple_of(c * size + parity * wide, wide), wide)
        start(("b", c), r.gb.at[part], r.gb.at[part], pair)

    def stage_out(c):
        arrived("b", c)
        for at in range(c * size // half, (c + 1) * size // half):
            rows = slice(at * half, (at + 1) * half)
            values = r.gb[rows].astype(F32)
            if at < 2 * slices:
                here = slice(at // 2 * half, (at // 2 + 1) * half)
                if at % 2 == 0:
                    r.out_e[:, here] = values
                else:
                    r.out_r[here] = values
            elif at == 2 * slices:
                r.out_p[...] = values
            else:
                s = at - 2 * slices - 1
                r.out_q[:, s * half:(s + 1) * half] = values

    stages = (stage_pair, stage_rest, stage_sum, stage_back, stage_out)
    stepped = [0]

    def tick():
        step = stepped[0]
        if step >= chunks + len(stages) - 1 or (step < chunks and step >= rowed[0]):
            return
        for k in reversed(range(len(stages))):
            if 0 <= step - k < chunks:
                stages[k](step - k)
        stepped[0] += 1

    homes, aways = (r.o_f, r.x_f), (r.y_b, r.z_b)
    r.small[...] = jnp.zeros_like(r.small)
    for q in range(slices):
        here = slice(q * half, (q + 1) * half)
        for b in (1, 0):
            cols = slice(b * hid + q * half, b * hid + (q + 1) * half)
            pre = dot(r.ln_two[:, :half], e_side[0][b][:, here]) + dot(
                r.ln_two[:, half:], e_side[1][b][:, here]
            )
            pre = pre + cvecs[b][2 + q:3 + q]
            erf_half = 0.5 * (1.0 + lax.erf(pre * ROOT_HALF))
            hidden = (pre * erf_half).astype(BF16)
            r.hidden[:, cols] = hidden
            slope = erf_half + pre * GAUSS_PEAK * jnp.exp(-0.5 * pre * pre)
            hgrad = dot_t(r.grad[:, :half], r_side[0][b][here]) + dot_t(
                r.grad[:, half:], r_side[1][b][here]
            )
            pgrad = (hgrad * slope).astype(BF16)
            r.pg[:, cols] = pgrad
            at = (32 if b == 0 else 16) + 2 + q
            r.small[at:at + 1] = jnp.sum(pgrad.astype(F32), axis=0, keepdims=True)
            up = slice(2 * q * half, (2 * q + 1) * half)
            down = slice((2 * q + 1) * half, (2 * q + 2) * half)
            for a, out in enumerate(homes if b == 0 else aways):
                side = slice(a * half, (a + 1) * half)
                out[up] = t_dot(r.ln_two[:, side], pgrad).astype(out.dtype)
                out[down] = t_dot(hidden, r.grad[:, side]).astype(out.dtype)
            if b == 1:
                away_done(2 * q + 2)
        home_done(2 * q + 2)
    second = jnp.concatenate(
        [
            dot_t(r.pg[:, :hid], e_side[a][0][...]) + dot_t(r.pg[:, hid:], e_side[a][1][...])
            for a in range(2)
        ],
        axis=1,
    )
    tick()
    mgrad = r.grad[...].astype(F32) + norm_backward(second, rvec[3:4], normed_two, inverse_two)
    r.mgrad[...] = mgrad
    r.mid_b[...] = mgrad.astype(BF16)
    for k, values in ((2, mgrad), (3, second * normed_two), (4, second), (5, r.grad[...].astype(F32))):
        total = jnp.sum(values, axis=0, keepdims=True)
        r.small[k:k + 1] = total[:, :half]
        r.small[8 + k:9 + k] = total[:, half:]
    base = 2 * slices * half
    for b in (1, 0):
        cols = slice(b * width, (b + 1) * width)
        r.mg[:, cols] = (
            dot_t(r.mid_b[:, :half], p_side[0][b][...]) + dot_t(r.mid_b[:, half:], p_side[1][b][...])
        ).astype(BF16)
        for a, out in enumerate(homes if b == 0 else aways):
            out[base:base + half] = t_dot(
                r.mixed[:, cols], r.mid_b[:, a * half:(a + 1) * half]
            ).astype(out.dtype)
    away_done(2 * slices + 1)

    def spread_out(key, values, out):
        tokens = t_dot(r.perm[...], values.astype(BF16)).astype(BF16)
        r.t_own[key] = tokens[:, :half]
        r.t_away[key] = tokens[:, half:]
        start(("o0", key), r.t_own.at[key], out.at[tokens_of(mine)], over_col)
        start(("o1", key), r.t_away.at[key], out.at[tokens_of(mine)], over_row)
        out[tokens_of(mine)] = tokens[:, :half]

    def pass_on(key, out):
        arrived("o1", key)
        start(("o2", key), out.at[tokens_of(theirs)], out.at[tokens_of(theirs)], over_col)

    def collect(key, out, result):
        arrived("o0", key)
        arrived("o2", key)
        result[...] = t_dot(r.sel[...], out[...]).astype(result.dtype)

    parts = [
        dot(r.hidden[:, :hid], r_side[a][0][...]) + dot(r.hidden[:, hid:], r_side[a][1][...])
        for a in range(2)
    ]
    home_done(2 * slices + 1)
    spread_out(0, r.middle[...] + jnp.concatenate(parts, axis=1) + rvec[5:6], r.t_blk)
    tick()

    for b in (1, 0):
        cols = slice(b * width, (b + 1) * width)
        small = 32 if b == 0 else 16
        q_sum = jnp.zeros((1, width), F32)
        v_sum = jnp.zeros((1, width), F32)
        for w in range(4):
            rows = slice(w * PAD, (w + 1) * PAD)
            keys, values = r.k[rows, cols], r.v[rows, cols]
            q_stack = stack_heads(r.q[rows, cols], mask)
            g_stack = stack_heads(r.mg[rows, cols], mask)
            probs = r.probs[b * 4 + w]
            pgrad = dot_t(g_stack, values)
            sgrad = probs * (pgrad - jnp.sum(probs * pgrad, axis=-1, keepdims=True))
            r.bg[b] = sgrad if w == 0 else r.bg[b] + sgrad
            score_b = sgrad.astype(BF16)
            q_grad = fold_heads(dot(score_b, keys), mask) * scale
            k_grad = t_dot(score_b, q_stack)
            v_grad = t_dot(probs.astype(BF16), g_stack)
            q_sum = q_sum + jnp.sum(q_grad, axis=0, keepdims=True)
            v_sum = v_sum + jnp.sum(v_grad, axis=0, keepdims=True)
            r.lin[b, rows, 0:width] = q_grad.astype(BF16)
            r.lin[b, rows, width:2 * width] = k_grad.astype(BF16)
            r.lin[b, rows, 2 * width:3 * width] = v_grad.astype(BF16)
            if w % 2 == 1:
                tick()
            if (b, w) == (1, 2):
                pass_on(0, r.t_blk)
        r.small[small:small + 1] = q_sum
        r.small[small + 1:small + 2] = v_sum
        for s in range(3):
            part = r.lin[b, :, s * width:(s + 1) * width]
            at = base + (s + 1) * half
            for a, out in enumerate(homes if b == 0 else aways):
                out[at:at + half] = t_dot(r.ln_one[:, a * half:(a + 1) * half], part).astype(out.dtype)
            if b == 1:
                away_done(2 * slices + 2 + s)
            else:
                home_done(2 * slices + 2 + s)
    tick()
    first = jnp.concatenate(
        [dot_t(r.lin[0], q_side[a][0][...]) + dot_t(r.lin[1], q_side[a][1][...]) for a in range(2)],
        axis=1,
    )
    for k, values in ((0, first * r.n_one[...]), (1, first)):
        total = jnp.sum(values, axis=0, keepdims=True)
        r.small[k:k + 1] = total[:, :half]
        r.small[8 + k:9 + k] = total[:, half:]
    for b in range(2):
        for k in range(0, WINDOW, 2):
            lines = [r.bg[b, pl.ds(k + i, heads, stride=PAD), :] for i in range(min(2, WINDOW - k))]
            r.flat[b * heads:(b + 1) * heads, k * PAD:(k + len(lines)) * PAD] = jnp.concatenate(lines, axis=1)
    table_grad = sum(dot_t(part, r.hot[...]) for part in thirds(r.flat[...]))
    r.small[40:48, 0:entries] = table_grad[:heads]
    r.small[24:32, 0:entries] = table_grad[heads:]
    start(("s0",), r.small.at[0:32], r.s_col, over_col)
    in_grad = r.mgrad[...] + norm_backward(first, rvec[0:1], r.n_one[...], inverse_one)
    spread_out(1, in_grad, r.t_in)
    tick()
    arrived("s0")
    r.s_mid[0:8] = r.small[8:16] + r.s_col[8:16]
    r.s_mid[8:24] = r.small[32:48] + r.s_col[16:32]
    start(("s1",), r.s_mid, r.s_row, over_row)
    collect(0, r.t_blk, r.out_b)
    tick()
    arrived("s1")
    r.s_pair[0:8] = r.small[0:8] + r.s_col[0:8] + r.s_row[0:8]
    r.s_pair[8:24] = r.s_mid[8:24] + r.s_row[8:24]
    start(("s2",), r.s_pair, r.s_other, pair)
    pass_on(1, r.t_in)
    tick()
    arrived("s2")
    r.s_dp[place] = r.s_pair[...] + r.s_other[...]
    for k in range(1, peers):
        start(("s3", k), r.s_dp.at[place], r.s_dp.at[place], peer_of(k)[1])
    tick()
    collect(1, r.t_in, r.out_x)
    tick()
    for k in range(1, peers):
        arrived("s3", k)
    acc = r.s_dp[0]
    for k in range(1, peers):
        acc = acc + r.s_dp[k]
    for k, ref in enumerate((r.o_gain1, r.o_shift1, r.o_bias_p, r.o_gain2, r.o_shift2, r.o_bias_r)):
        ref[...] = acc[k:k + 1]
    r.o_bias_q[...] = acc[8:9]
    r.o_bias_v[...] = acc[9:10]
    for k in range(slices):
        r.o_bias_e[:, k * half:(k + 1) * half] = acc[10 + k:11 + k]
    unit = jnp.where(
        lax.broadcasted_iota(jnp.int32, (heads, heads), 0)
        == lax.broadcasted_iota(jnp.int32, (heads, heads), 1),
        1.0,
        0.0,
    ).astype(BF16)
    turned = sum(t_dot(part, unit) for part in thirds(acc[16:16 + heads]))
    r.o_table[...] = turned[:entries]
    while stepped[0] < chunks + len(stages) - 1:
        tick()
    for key, copy in live.items():
        copy.wait_send()


def per_device(
    block_input, out_grad, first_gain, first_shift, qkv_weight, query_bias, value_bias,
    position_table, position_index, proj_weight, proj_bias, second_gain, second_shift,
    expand_weight, expand_bias, reduce_weight, reduce_bias,
):
    n = lax.axis_size("dp")
    half = block_input.shape[1]
    width = qkv_weight.shape[2]
    hid = expand_weight.shape[1]
    entries, heads = position_table.shape
    images = block_input.shape[0] // IMAGE
    full = 2 * half
    rows = 2 * hid + 4 * half
    size = max(n * 16, half)
    chunks, peers, wide = rows // size, n // 2, size // 2
    index = jnp.pad(position_index, ((0, 0), (0, PAD - WINDOW)), constant_values=-1).reshape(1, -1)
    inputs = dict(
        x_in=block_input, g_in=out_grad,
        gain1=first_gain[None], shift1=first_shift[None], bias_p=proj_bias[None],
        gain2=second_gain[None], shift2=second_shift[None], bias_r=reduce_bias[None],
        bias_q=query_bias[None], bias_v=value_bias[None], bias_e=expand_bias[None],
        table=position_table, index=index,
        wq=qkv_weight.reshape(half, 3 * width), wp=proj_weight, we=expand_weight, wr=reduce_weight,
    )
    outputs = dict(
        out_b=(block_input.shape, BF16), out_x=(block_input.shape, F32),
        out_q=((half, 3 * width), F32), out_p=((width, half), F32),
        out_e=((half, hid), F32), out_r=((hid, half), F32),
        o_gain1=((1, half), F32), o_shift1=((1, half), F32), o_bias_p=((1, half), F32),
        o_gain2=((1, half), F32), o_shift2=((1, half), F32), o_bias_r=((1, half), F32),
        o_bias_q=((1, width), F32), o_bias_v=((1, width), F32), o_bias_e=((1, hid), F32),
        o_table=((entries, heads), F32),
    )
    scratch = dict(
        sel=((images * TOK, images * IMAGE), BF16), perm=((ROWS, TOK), BF16),
        x_away=((TOK, half), BF16), x_oth=((TOK, half), BF16),
        g_away=((TOK, half), BF16), g_oth=((TOK, half), BF16),
        vec_own=((8, half), F32), vec_oth=((8, half), F32),
        cvec_own=((8, half), F32), cvec_oth=((8, half), F32),
        hot=((entries, WINDOW * PAD), BF16),
        b_own=((heads * PAD, PAD), F32), b_oth=((heads * PAD, PAD), F32),
        n_one=((ROWS, full), F32), ln_one=((ROWS, full), BF16),
        q=((ROWS, full), BF16), k=((ROWS, full), BF16), v=((ROWS, full), BF16),
        mixed=((ROWS, full), BF16), probs=((8, heads * PAD, PAD), F32),
        middle=((ROWS, full), F32), ln_two=((ROWS, full), BF16), grad=((ROWS, full), BF16),
        hidden=((ROWS, 2 * hid), BF16), pg=((ROWS, 2 * hid), BF16),
        mgrad=((ROWS, full), F32), mid_b=((ROWS, full), BF16), mg=((ROWS, full), BF16),
        lin=((2, ROWS, 3 * width), BF16), bg=((2, heads * PAD, PAD), F32),
        flat=((2 * heads, WINDOW * PAD), F32),
        t_own=((2, TOK, half), BF16), t_away=((2, TOK, half), BF16),
        t_blk=((images * TOK, half), BF16), t_in=((images * TOK, half), BF16),
        o_f=((rows, half), F32), x_f=((rows, half), F32),
        y_b=((rows, half), BF16), z_b=((rows, half), BF16),
        yr=((rows, half), BF16), zr=((rows, half), BF16),
        xb=((rows, half), BF16), xr=((rows, half), BF16), sb=((rows, half), BF16),
        gb=((rows, half), BF16), sf=((size, half), F32),
        pr=((chunks, wide, half), BF16), tb=((chunks, wide, half), BF16),
        tf=((chunks, wide, half), F32), qr=((chunks, peers, size // n, half), BF16),
        small=((48, half), F32), s_col=((32, half), F32), s_mid=((24, half), F32),
        s_row=((24, half), F32), s_pair=((24, half), F32), s_other=((24, half), F32),
        s_dp=((peers, 24, half), F32),
    )
    for name, weight in (("q", "wq"), ("p", "wp"), ("e", "we"), ("r", "wr")):
        for side in ("xo", "ox", "xx"):
            scratch[name + "_" + side] = (inputs[weight].shape, BF16)
    copies = 64 + chunks * (5 + 2 * (peers - 1)) + peers
    names = list(inputs) + list(outputs) + list(scratch) + ["sems"]
    results = pl.pallas_call(
        functools.partial(block_kernel, n, size, names),
        name="block",
        out_shape=tuple(jax.ShapeDtypeStruct(*out) for out in outputs.values()),
        in_specs=[VMEM] * len(inputs),
        out_specs=tuple([VMEM] * len(outputs)),
        scratch_shapes=[pltpu.VMEM(*shape) for shape in scratch.values()]
        + [pltpu.SemaphoreType.DMA((2, copies))],
        compiler_params=pltpu.CompilerParams(
            collective_id=0, has_side_effects=True, vmem_limit_bytes=LIMIT
        ),
    )(*inputs.values())
    got = dict(zip(outputs, results))
    return (
        got["out_b"], got["out_x"], got["o_gain1"][0], got["o_shift1"][0],
        got["out_q"].reshape(half, 3, width), got["o_bias_q"][0], got["o_bias_v"][0],
        got["o_table"], got["out_p"], got["o_bias_p"][0], got["o_gain2"][0], got["o_shift2"][0],
        got["out_e"], got["o_bias_e"][0], got["out_r"], got["o_bias_r"][0],
    )


def solution(mesh):
    in_specs = (
        P("dp", "row"), P("dp", "row"), P("row"), P("row"), P("row", None, "col"), P("col"),
        P("col"), P(None, "col"), P(), P("col", "row"), P("row"), P("row"), P("row"),
        P("row", "col"), P("col"), P("col", "row"), P("row"),
    )
    out_specs = (
        P("dp", "row"), P("dp", "row"), P("row"), P("row"), P("row", None, "col"), P("col"),
        P("col"), P(None, "col"), P("col", "row"), P("row"), P("row"), P("row"),
        P("row", "col"), P("col"), P("col", "row"), P("row"),
    )
    return jax.shard_map(
        per_device, mesh=mesh, in_specs=in_specs, out_specs=out_specs, check_vma=False
    )
```

profile of v0, /device:TPU:0, one launch (start us, length us, event | category | flops | bytes accessed | tf_op | source)
XLA Modules:
  0.0 149.8 jit_solution(5686540275209793504)
XLA Ops:
  0.6 0.8 pad.4
  1.4 0.7 reshape.41.refs_12_
  2.1 0.7 copy.38.refs_11_
  2.8 1.2 copy.37
  4.0 0.9 copy.39.refs_13_
  4.9 130.8 %block.1 = (bf16[784,256]{1,0:T(8,128)(2,1)}, f32[784,256]{1,0:T(8,128)}, f32[256,768]{1,0:T(8,128)}, f32[256,256]{1,0:T(8,128)}, f32[256,1024]{1,0:T(8,128)}, /...) custom-call(bf16[784,256]{1,0:T(8,128)(2,1)} %refs_0_.1, ...), custom_call_target="tpu_custom_call" | custom-call | tf_op jit(solution)/shard_map/block/pallas_call | solution.py:611
  135.8 1.6 %copy.42 = f32[169,8]{0,1:T(8,128)} copy(f32[169,8]{1,0:T(8,128)} %get-tuple-element.71) | data formatting | bytes 10816
  137.3 1.4 copy.40
  138.8 1.1 copy.41
  139.9 0.7 copy.57
  140.7 0.9 copy.58
  141.6 0.6 copy.59
  142.2 0.6 copy.60
  142.8 0.1 copy-done.12
  142.9 0.6 copy.61
  143.6 0.6 copy.62
  144.1 0.7 copy.63
  144.8 0.6 copy.64
  145.5 0.6 copy.65
  146.1 0.6 copy.66
  146.7 1.0 copy.67
  147.7 0.6 copy.68
  148.3 1.0 copy.69
  149.3 0.6 copy.70
  (29 shorter events, 0.4 us)
Async XLA Ops:
  1.4 0.7 copy-start.5
  138.7 1.2 copy-start.3
  138.8 1.9 %copy-start.2 = (f32[784,256]{1,0:T(8,128)S(1)}, f32[784,256]{1,0:T(8,128)}, u32[]{:S(2)}) copy-start(f32[784,256]{1,0:T(8,128)} %get-tuple-element.97) | copy-start | bytes 2408452
  140.7 0.9 copy-start.14
  140.7 3.5 %copy-start.4 = (f32[256,256]{1,0:T(8,128)S(1)}, f32[256,256]{1,0:T(8,128)}, u32[]{:S(2)}) copy-start(f32[256,256]{1,0:T(8,128)} %get-tuple-element.104) | copy-start | bytes 786436
  140.7 6.0 %copy-start.1 = (f32[256,1024]{1,0:T(8,128)S(1)}, f32[256,1024]{1,0:T(8,128)}, u32[]{:S(2)}) copy-start(f32[256,1024]{1,0:T(8,128)} %get-tuple-element.108) | copy-start | bytes 3145732
  141.6 0.7 copy-start.13
  142.2 0.7 copy-start.12
  142.9 0.7 copy-start.11
  144.1 0.7 copy-start.10
  144.8 0.7 copy-start.9
  145.5 0.6 copy-start.8
  146.7 1.0 copy-start.6
  146.7 1.6 %copy-start = (f32[1024,256]{1,0:T(8,128)S(1)}, f32[1024,256]{1,0:T(8,128)}, u32[]{:S(2)}) copy-start(f32[1024,256]{1,0:T(8,128)} %get-tuple-element.110) | copy-start | bytes 3145732
  148.3 1.0 copy-start.7
where the time goes:
time: 150 us
  Pallas kernels  131 us (87%)
  local copies, waits for them, and re-layouts  18.3 us (12%)
    pallas_call x1, Pallas kernels, per_device(): pl.pallas_call(functools.partial(block_kernel, n, size, names), name='blo...  131 us
    unnamed x48, local copies, waits for them, and re-layouts  14.5 us

commit v1 on v0

--- a/solution.py
+++ b/solution.py
@@ -16,6 +16,7 @@
 IMAGE = 4 * WINDOW
 TOK = 208
 PAD = 64
+LANES = 128
 ROWS = 4 * PAD
 F32 = jnp.float32
 BF16 = jnp.bfloat16
@@ -37,10 +38,15 @@
 
 
 def thirds(values):
-    high = values.astype(BF16)
-    rest = values - high.astype(F32)
-    middle = rest.astype(BF16)
-    return high, middle, (rest - middle.astype(F32)).astype(BF16)
+    high = values.astype(BF16).astype(F32)
+    rest = values - high
+    middle = rest.astype(BF16).astype(F32)
+    return jnp.concatenate([high, middle, rest - middle], axis=0).astype(BF16)
+
+
+def unthird(values):
+    count = values.shape[0] // 3
+    return values[:count] + values[count:2 * count] + values[2 * count:]
 
 
 def norm(values):
@@ -95,11 +101,10 @@
     over_col, over_row = {"col": 1 - col}, {"row": 1 - row}
     pair = {"dp": me + 1 - 2 * parity}
     half, width, hid = r.x_in.shape[1], r.wp.shape[0], r.we.shape[1]
-    heads = r.table.shape[1]
+    heads, entries = r.table.shape
     scale = (width // heads) ** (-0.5)
     images = r.x_in.shape[0] // IMAGE
     slices = hid // half
-    full = 2 * half
     mine = row * cores + col
     theirs = (1 - row) * cores + col
     wide, block = size // 2, size // n
@@ -127,6 +132,81 @@
     def tokens_of(image):
         return pl.ds(pl.multiple_of(image * TOK, 16), TOK)
 
+    r.vec_own[...] = jnp.zeros_like(r.vec_own)
+    r.cvec_own[...] = jnp.zeros_like(r.cvec_own)
+    for k, ref in enumerate((r.gain1, r.shift1, r.bias_p, r.gain2, r.shift2, r.bias_r)):
+        r.vec_own[k:k + 1] = ref[...]
+    r.cvec_own[0:1] = r.bias_q[...]
+    r.cvec_own[1:2] = r.bias_v[...]
+    for k in range(slices):
+        r.cvec_own[2 + k:3 + k] = r.bias_e[:, k * half:(k + 1) * half]
+    pl.semaphore_wait(barrier, peers + 2)
+
+    above = lax.rem(place, 2)
+    along = {"dp": 2 * (place + 1 - 2 * above) + parity}
+    weights = {
+        "q": (r.wq, r.q_xo, r.q_ox, r.q_xx, 2, "x"),
+        "p": (r.wp, r.p_xo, r.p_ox, r.p_xx, 1, "z"),
+        "e": (r.we, r.e_xo, r.e_ox, r.e_xx, 2, "z"),
+        "r": (r.wr, r.r_xo, r.r_ox, r.r_xx, 2, "x"),
+    }
+
+    def view(name, ref, kind, p):
+        count = weights[name][4]
+        rows = ref.shape[-2]
+        step = rows // (4 * count)
+        quarter = {
+            "y": 2 * above + parity,
+            "x": 2 * above + 1 - parity,
+            "z": 2 * (1 - above) + parity,
+            "d": 2 * (1 - above) + 1 - parity,
+        }[kind]
+        at = pl.ds(pl.multiple_of(quarter * (rows // 4) + p * step, step), step)
+        return ref.at[:, at] if len(ref.shape) == 3 else ref.at[at]
+
+    def fetch(name):
+        oo, xo, ox = weights[name][:3]
+        for p in range(weights[name][4]):
+            start((name, "y", p), view(name, oo, "y", p), view(name, xo, "y", p), over_row)
+        start((name, "c"), oo, ox, over_col)
+
+    def across(name, kind, p):
+        arrived(name, kind, p)
+        xo, xx = weights[name][1], weights[name][3]
+        start((name, "c" + kind, p), view(name, xo, kind, p), view(name, xx, kind, p), over_col)
+
+    def relay_one(name):
+        xo = weights[name][1]
+        for p in range(weights[name][4]):
+            own = view(name, xo, "y", p)
+            arrived(name, "y", p)
+            start((name, "x", p), own, own, pair)
+            start((name, "z", p), own, own, along)
+            start((name, "cy", p), own, view(name, weights[name][3], "y", p), over_col)
+
+    def relay_two(name):
+        first = weights[name][5]
+        for p in range(weights[name][4]):
+            got = view(name, weights[name][1], first, p)
+            arrived(name, first, p)
+            start((name, "d", p), got, got, along if first == "x" else pair)
+            start((name, "c" + first, p), got, view(name, weights[name][3], first, p), over_col)
+
+    def relay_three(name):
+        second = "z" if weights[name][5] == "x" else "x"
+        for kind in (second, "d"):
+            for p in range(weights[name][4]):
+                across(name, kind, p)
+
+    def ready(name):
+        arrived(name, "c")
+        for kind in ("cy", "cx", "cz", "cd"):
+            for p in range(weights[name][4]):
+                arrived(name, kind, p)
+
+    fetch("q")
+    start(("vec",), r.vec_own, r.vec_oth, over_row)
+    start(("cvec",), r.cvec_own, r.cvec_oth, over_col)
     spot = lax.broadcasted_iota(jnp.int32, (TOK, images * IMAGE), 1)
     line = lax.broadcasted_iota(jnp.int32, (TOK, images * IMAGE), 0)
     line = jnp.where(line < IMAGE, line, -IMAGE * images)
@@ -141,75 +221,25 @@
     r.perm[...] = jnp.where(spot == target, 1.0, 0.0).astype(BF16)
     sel_mine, sel_theirs = r.sel[tokens_of(mine)], r.sel[tokens_of(theirs)]
     r.x_away[...] = dot(sel_theirs, r.x_in[...]).astype(BF16)
-    r.g_away[...] = dot(sel_theirs, r.g_in[...]).astype(BF16)
-    r.vec_own[...] = jnp.zeros_like(r.vec_own)
-    r.cvec_own[...] = jnp.zeros_like(r.cvec_own)
-    for k, ref in enumerate((r.gain1, r.shift1, r.bias_p, r.gain2, r.shift2, r.bias_r)):
-        r.vec_own[k:k + 1] = ref[...]
-    r.cvec_own[0:1] = r.bias_q[...]
-    r.cvec_own[1:2] = r.bias_v[...]
-    for k in range(slices):
-        r.cvec_own[2 + k:3 + k] = r.bias_e[:, k * half:(k + 1) * half]
-    pl.semaphore_wait(barrier, peers + 2)
-
-    weights = {
-        "q": (r.wq, r.q_xo, r.q_ox, r.q_xx, 2),
-        "p": (r.wp, r.p_xo, r.p_ox, r.p_xx, 1),
-        "e": (r.we, r.e_xo, r.e_ox, r.e_xx, 2),
-        "r": (r.wr, r.r_xo, r.r_ox, r.r_xx, 2),
-    }
-
-    def pieces(name, side):
-        rows, count = weights[name][0].shape[0], weights[name][4]
-        step = rows // (2 * count)
-        for p in range(count):
-            yield p, pl.ds(pl.multiple_of(side * (rows // 2) + p * step, step), step)
-
-    def fetch(name):
-        oo, xo, ox, _, _ = weights[name]
-        for p, rows in pieces(name, parity):
-            start((name, "y", p), oo.at[rows], xo.at[rows], over_row)
-        start((name, "c"), oo, ox, over_col)
-
-    def relay(name):
-        _, xo, _, xx, _ = weights[name]
-        for p, rows in pieces(name, parity):
-            arrived(name, "y", p)
-            start((name, "x", p), xo.at[rows], xo.at[rows], pair)
-            start((name, "cy", p), xo.at[rows], xx.at[rows], over_col)
-
-    def relay_back(name):
-        _, xo, _, xx, _ = weights[name]
-        for p, rows in pieces(name, 1 - parity):
-            arrived(name, "x", p)
-            start((name, "cx", p), xo.at[rows], xx.at[rows], over_col)
-
-    def ready(name):
-        arrived(name, "c")
-        for p in range(weights[name][4]):
-            arrived(name, "cy", p)
-            arrived(name, "cx", p)
-
     start(("x",), r.x_away, r.x_oth, over_row)
-    start(("vec",), r.vec_own, r.vec_oth, over_row)
-    start(("cvec",), r.cvec_own, r.cvec_oth, over_col)
-    fetch("q")
     fetch("p")
     fetch("e")
+    fetch("r")
+    r.g_away[...] = dot(sel_theirs, r.g_in[...]).astype(BF16)
     start(("g",), r.g_away, r.g_oth, over_row)
-    fetch("r")
-
-    entries = r.table.shape[0]
-    which = lax.broadcasted_iota(jnp.int32, (entries, WINDOW * PAD), 0)
-    r.hot[...] = jnp.where(which == r.index[...], 1.0, 0.0).astype(BF16)
-    spread = sum(t_dot(part, r.hot[...]) for part in thirds(r.table[...]))
+    which = lax.broadcasted_iota(jnp.int32, (entries, LANES), 0)
+    for k in range(WINDOW):
+        r.hot[:, k * LANES:(k + 1) * LANES] = jnp.where(which == r.index[k:k + 1], 1.0, 0.0).astype(BF16)
+    relay_one("q")
+    spread = unthird(dot(thirds(r.table[...]), r.hot[...]))
     lane = lax.broadcasted_iota(jnp.int32, (heads, PAD), 1)
     r.b_own[...] = jnp.zeros_like(r.b_own)
     for k in range(WINDOW):
         r.b_own[pl.ds(k, heads, stride=PAD), :] = jnp.where(
-            lane < WINDOW, spread[:, k * PAD:(k + 1) * PAD], -1e30
+            lane < WINDOW, spread[:, k * LANES:k * LANES + PAD], -1e30
         )
     start(("bias",), r.b_own, r.b_oth, over_col)
+    relay_two("q")
     x_own = dot(sel_mine, r.x_in[...]).astype(BF16)
     grad_own = dot(sel_mine, r.g_in[...]).astype(BF16)
     mask = head_mask(heads, width)
@@ -221,9 +251,9 @@
     normed, inverse_one = norm(x)
     r.n_one[...] = normed
     r.ln_one[...] = (normed * rvec[0:1] + rvec[1:2]).astype(BF16)
-    relay("q")
-    relay_back("q")
-    relay("p")
+    relay_one("p")
+    relay_three("q")
+    relay_two("p")
     arrived("cvec")
     q_side = (r.wq, r.q_ox), (r.q_xo, r.q_xx)
     p_side = (r.wp, r.p_ox), (r.p_xo, r.p_xx)
@@ -231,16 +261,16 @@
     r_side = (r.wr, r.r_ox), (r.r_xo, r.r_xx)
     bias_refs = (r.b_own, r.b_oth)
     cvecs = (r.cvec_own, r.cvec_oth)
-    step_of = {(0, 1): ("relay_back", "p"), (0, 3): ("relay", "e"), (1, 1): ("relay_back", "e"), (1, 2): ("relay", "r")}
     for b in range(2):
         cols = slice(b * width, (b + 1) * width)
         if b == 1:
+            relay_three("p")
+            relay_one("e")
             ready("q")
             arrived("bias")
         for s, out in enumerate((r.q, r.k, r.v)):
-            part = slice(s * width, (s + 1) * width)
-            linear = dot(r.ln_one[:, :half], q_side[0][b][:, part]) + dot(
-                r.ln_one[:, half:], q_side[1][b][:, part]
+            linear = dot(r.ln_one[:, :half], q_side[0][b][s]) + dot(
+                r.ln_one[:, half:], q_side[1][b][s]
             )
             if s == 0:
                 linear = (linear + cvecs[b][0:1]) * scale
@@ -253,9 +283,8 @@
             probs = softmax(scores)
             r.probs[b * 4 + w] = probs
             r.mixed[rows, cols] = fold_heads(dot(probs.astype(BF16), r.v[rows, cols]), mask).astype(BF16)
-            if (b, w) in step_of:
-                what, name = step_of[b, w]
-                (relay if what == "relay" else relay_back)(name)
+    relay_two("e")
+    relay_one("r")
     ready("p")
     parts = [
         dot(r.mixed[:, :width], p_side[a][0][...]) + dot(r.mixed[:, width:], p_side[a][1][...])
@@ -265,10 +294,12 @@
     r.middle[...] = middle
     normed_two, inverse_two = norm(middle)
     r.ln_two[...] = (normed_two * rvec[3:4] + rvec[4:5]).astype(BF16)
-    relay_back("r")
+    relay_three("e")
+    relay_two("r")
     arrived("g")
     grad = dot(r.perm[...], jnp.concatenate([grad_own, r.g_oth[...]], axis=1))
     r.grad[...] = grad.astype(BF16)
+    relay_three("r")
     ready("e")
     ready("r")
 
@@ -330,32 +361,21 @@
 
     def stage_out(c):
         arrived("b", c)
-        for at in range(c * size // half, (c + 1) * size // half):
-            rows = slice(at * half, (at + 1) * half)
-            values = r.gb[rows].astype(F32)
-            if at < 2 * slices:
-                here = slice(at // 2 * half, (at // 2 + 1) * half)
-                if at % 2 == 0:
-                    r.out_e[:, here] = values
-                else:
-                    r.out_r[here] = values
-            elif at == 2 * slices:
-                r.out_p[...] = values
-            else:
-                s = at - 2 * slices - 1
-                r.out_q[:, s * half:(s + 1) * half] = values
-
+
+    drain = 2.9 * size / 256
+    hop = 1.8 + drain / 2
     stages = (stage_pair, stage_rest, stage_sum, stage_back, stage_out)
-    stepped = [0]
-
-    def tick():
-        step = stepped[0]
-        if step >= chunks + len(stages) - 1 or (step < chunks and step >= rowed[0]):
-            return
-        for k in reversed(range(len(stages))):
-            if 0 <= step - k < chunks:
-                stages[k](step - k)
-        stepped[0] += 1
+    pending = sorted(
+        (2.6 + drain * (c + 1) + hop * k, c, k) for c in range(chunks) for k in range(len(stages))
+    )
+
+    def advance(until):
+        while pending and pending[0][0] <= until:
+            _, c, k = pending[0]
+            if k == 0 and c >= rowed[0]:
+                return
+            stages[k](c)
+            pending.pop(0)
 
     homes, aways = (r.o_f, r.x_f), (r.y_b, r.z_b)
     r.small[...] = jnp.zeros_like(r.small)
@@ -387,6 +407,7 @@
             if b == 1:
                 away_done(2 * q + 2)
         home_done(2 * q + 2)
+    advance(6.5)
     second = jnp.concatenate(
         [
             dot_t(r.pg[:, :hid], e_side[a][0][...]) + dot_t(r.pg[:, hid:], e_side[a][1][...])
@@ -394,7 +415,6 @@
         ],
         axis=1,
     )
-    tick()
     mgrad = r.grad[...].astype(F32) + norm_backward(second, rvec[3:4], normed_two, inverse_two)
     r.mgrad[...] = mgrad
     r.mid_b[...] = mgrad.astype(BF16)
@@ -437,7 +457,7 @@
     ]
     home_done(2 * slices + 1)
     spread_out(0, r.middle[...] + jnp.concatenate(parts, axis=1) + rvec[5:6], r.t_blk)
-    tick()
+    advance(9)
 
     for b in (1, 0):
         cols = slice(b * width, (b + 1) * width)
@@ -462,10 +482,6 @@
             r.lin[b, rows, 0:width] = q_grad.astype(BF16)
             r.lin[b, rows, width:2 * width] = k_grad.astype(BF16)
             r.lin[b, rows, 2 * width:3 * width] = v_grad.astype(BF16)
-            if w % 2 == 1:
-                tick()
-            if (b, w) == (1, 2):
-                pass_on(0, r.t_blk)
         r.small[small:small + 1] = q_sum
         r.small[small + 1:small + 2] = v_sum
         for s in range(3):
@@ -477,68 +493,103 @@
                 away_done(2 * slices + 2 + s)
             else:
                 home_done(2 * slices + 2 + s)
-    tick()
+        advance(12 if b == 1 else 15)
     first = jnp.concatenate(
-        [dot_t(r.lin[0], q_side[a][0][...]) + dot_t(r.lin[1], q_side[a][1][...]) for a in range(2)],
+        [
+            sum(
+                dot_t(r.lin[b, :, s * width:(s + 1) * width], q_side[a][b][s])
+                for b in range(2)
+                for s in range(3)
+            )
+            for a in range(2)
+        ],
         axis=1,
     )
     for k, values in ((0, first * r.n_one[...]), (1, first)):
         total = jnp.sum(values, axis=0, keepdims=True)
         r.small[k:k + 1] = total[:, :half]
         r.small[8 + k:9 + k] = total[:, half:]
+    r.flat[...] = jnp.zeros_like(r.flat)
     for b in range(2):
-        for k in range(0, WINDOW, 2):
-            lines = [r.bg[b, pl.ds(k + i, heads, stride=PAD), :] for i in range(min(2, WINDOW - k))]
-            r.flat[b * heads:(b + 1) * heads, k * PAD:(k + len(lines)) * PAD] = jnp.concatenate(lines, axis=1)
-    table_grad = sum(dot_t(part, r.hot[...]) for part in thirds(r.flat[...]))
+        for k in range(WINDOW):
+            r.flat[b * heads:(b + 1) * heads, k * LANES:k * LANES + PAD] = r.bg[
+                b, pl.ds(k, heads, stride=PAD), :
+            ]
+    table_grad = unthird(dot_t(thirds(r.flat[...]), r.hot[...]))
     r.small[40:48, 0:entries] = table_grad[:heads]
     r.small[24:32, 0:entries] = table_grad[heads:]
     start(("s0",), r.small.at[0:32], r.s_col, over_col)
     in_grad = r.mgrad[...] + norm_backward(first, rvec[0:1], r.n_one[...], inverse_one)
     spread_out(1, in_grad, r.t_in)
-    tick()
+    advance(18)
+    pass_on(0, r.t_blk)
     arrived("s0")
     r.s_mid[0:8] = r.small[8:16] + r.s_col[8:16]
     r.s_mid[8:24] = r.small[32:48] + r.s_col[16:32]
     start(("s1",), r.s_mid, r.s_row, over_row)
+    advance(22)
     collect(0, r.t_blk, r.out_b)
-    tick()
+    late = 2.6 + drain * chunks
+    advance(late)
     arrived("s1")
     r.s_pair[0:8] = r.small[0:8] + r.s_col[0:8] + r.s_row[0:8]
     r.s_pair[8:24] = r.s_mid[8:24] + r.s_row[8:24]
     start(("s2",), r.s_pair, r.s_other, pair)
+    advance(late + 3.5)
     pass_on(1, r.t_in)
-    tick()
     arrived("s2")
     r.s_dp[place] = r.s_pair[...] + r.s_other[...]
     for k in range(1, peers):
         start(("s3", k), r.s_dp.at[place], r.s_dp.at[place], peer_of(k)[1])
-    tick()
+    advance(late + 7)
     collect(1, r.t_in, r.out_x)
-    tick()
     for k in range(1, peers):
         arrived("s3", k)
     acc = r.s_dp[0]
     for k in range(1, peers):
         acc = acc + r.s_dp[k]
-    for k, ref in enumerate((r.o_gain1, r.o_shift1, r.o_bias_p, r.o_gain2, r.o_shift2, r.o_bias_r)):
-        ref[...] = acc[k:k + 1]
-    r.o_bias_q[...] = acc[8:9]
-    r.o_bias_v[...] = acc[9:10]
-    for k in range(slices):
-        r.o_bias_e[:, k * half:(k + 1) * half] = acc[10 + k:11 + k]
-    unit = jnp.where(
-        lax.broadcasted_iota(jnp.int32, (heads, heads), 0)
-        == lax.broadcasted_iota(jnp.int32, (heads, heads), 1),
-        1.0,
-        0.0,
-    ).astype(BF16)
-    turned = sum(t_dot(part, unit) for part in thirds(acc[16:16 + heads]))
-    r.o_table[...] = turned[:entries]
-    while stepped[0] < chunks + len(stages) - 1:
-        tick()
+    r.sums[...] = acc
+    advance(1e9)
     for key, copy in live.items():
         copy.wait_send()
+
+
+def deliver_kernel(slices, gb, out_b, out_x, sums, *refs):
+    outs, sems = refs[:16], refs[-1]
+    held = refs[16:-1]
+    half = gb.shape[1]
+    copies = []
+
+    def send(at, src, dst):
+        copies.append(pltpu.make_async_copy(src, dst, sems.at[at]))
+        copies[-1].start()
+
+    send(0, out_b, outs[0])
+    for q in range(slices):
+        cols = slice(q * half, (q + 1) * half)
+        held[0][:, cols] = gb[2 * q * half:(2 * q + 1) * half].astype(F32)
+    send(1, held[0], outs[12])
+    for q in range(slices):
+        held[1][q * half:(q + 1) * half] = gb[(2 * q + 1) * half:(2 * q + 2) * half].astype(F32)
+    send(2, held[1], outs[14])
+    held[2][...] = out_x[...].astype(F32)
+    send(3, held[2], outs[1])
+    base = 2 * slices * half
+    for s in range(3):
+        held[3][s] = gb[base + (s + 1) * half:base + (s + 2) * half].astype(F32)
+    send(4, held[3], outs[4])
+    held[4][...] = gb[base:base + half].astype(F32)
+    send(5, held[4], outs[8])
+    for k, at in enumerate((2, 3, 9, 10, 11, 15)):
+        outs[at][...] = sums[k:k + 1]
+    outs[5][...] = sums[8:9]
+    outs[6][...] = sums[9:10]
+    for k in range(slices):
+        outs[13][:, k * half:(k + 1) * half] = sums[10 + k:11 + k]
+    heads, entries = outs[7].shape
+    outs[7][...] = sums[16:16 + heads, 0:entries]
+    for copy in copies:
+        copy.wait()
 
 
 def per_device(
@@ -551,28 +602,24 @@
     width = qkv_weight.shape[2]
     hid = expand_weight.shape[1]
     entries, heads = position_table.shape
+    slices = hid // half
     images = block_input.shape[0] // IMAGE
     full = 2 * half
     rows = 2 * hid + 4 * half
     size = max(n * 16, half)
     chunks, peers, wide = rows // size, n // 2, size // 2
-    index = jnp.pad(position_index, ((0, 0), (0, PAD - WINDOW)), constant_values=-1).reshape(1, -1)
+    index = jnp.pad(position_index, ((0, 0), (0, LANES - WINDOW)), constant_values=-1)
     inputs = dict(
         x_in=block_input, g_in=out_grad,
         gain1=first_gain[None], shift1=first_shift[None], bias_p=proj_bias[None],
         gain2=second_gain[None], shift2=second_shift[None], bias_r=reduce_bias[None],
         bias_q=query_bias[None], bias_v=value_bias[None], bias_e=expand_bias[None],
-        table=position_table, index=index,
-        wq=qkv_weight.reshape(half, 3 * width), wp=proj_weight, we=expand_weight, wr=reduce_weight,
+        table=position_table.T, index=index,
+        wq=qkv_weight.transpose(1, 0, 2), wp=proj_weight, we=expand_weight, wr=reduce_weight,
     )
     outputs = dict(
-        out_b=(block_input.shape, BF16), out_x=(block_input.shape, F32),
-        out_q=((half, 3 * width), F32), out_p=((width, half), F32),
-        out_e=((half, hid), F32), out_r=((hid, half), F32),
-        o_gain1=((1, half), F32), o_shift1=((1, half), F32), o_bias_p=((1, half), F32),
-        o_gain2=((1, half), F32), o_shift2=((1, half), F32), o_bias_r=((1, half), F32),
-        o_bias_q=((1, width), F32), o_bias_v=((1, width), F32), o_bias_e=((1, hid), F32),
-        o_table=((entries, heads), F32),
+        gb=((rows, half), BF16), out_b=(block_input.shape, BF16), out_x=(block_input.shape, BF16),
+        sums=((24, half), F32),
     )
     scratch = dict(
         sel=((images * TOK, images * IMAGE), BF16), perm=((ROWS, TOK), BF16),
@@ -580,7 +627,7 @@
         g_away=((TOK, half), BF16), g_oth=((TOK, half), BF16),
         vec_own=((8, half), F32), vec_oth=((8, half), F32),
         cvec_own=((8, half), F32), cvec_oth=((8, half), F32),
-        hot=((entries, WINDOW * PAD), BF16),
+        hot=((entries, WINDOW * LANES), BF16),
         b_own=((heads * PAD, PAD), F32), b_oth=((heads * PAD, PAD), F32),
         n_one=((ROWS, full), F32), ln_one=((ROWS, full), BF16),
         q=((ROWS, full), BF16), k=((ROWS, full), BF16), v=((ROWS, full), BF16),
@@ -589,14 +636,14 @@
         hidden=((ROWS, 2 * hid), BF16), pg=((ROWS, 2 * hid), BF16),
         mgrad=((ROWS, full), F32), mid_b=((ROWS, full), BF16), mg=((ROWS, full), BF16),
         lin=((2, ROWS, 3 * width), BF16), bg=((2, heads * PAD, PAD), F32),
-        flat=((2 * heads, WINDOW * PAD), F32),
+        flat=((2 * heads, WINDOW * LANES), F32),
         t_own=((2, TOK, half), BF16), t_away=((2, TOK, half), BF16),
         t_blk=((images * TOK, half), BF16), t_in=((images * TOK, half), BF16),
         o_f=((rows, half), F32), x_f=((rows, half), F32),
         y_b=((rows, half), BF16), z_b=((rows, half), BF16),
         yr=((rows, half), BF16), zr=((rows, half), BF16),
         xb=((rows, half), BF16), xr=((rows, half), BF16), sb=((rows, half), BF16),
-        gb=((rows, half), BF16), sf=((size, half), F32),
+        sf=((size, half), F32),
         pr=((chunks, wide, half), BF16), tb=((chunks, wide, half), BF16),
         tf=((chunks, wide, half), F32), qr=((chunks, peers, size // n, half), BF16),
         small=((48, half), F32), s_col=((32, half), F32), s_mid=((24, half), F32),
@@ -606,7 +653,7 @@
     for name, weight in (("q", "wq"), ("p", "wp"), ("e", "we"), ("r", "wr")):
         for side in ("xo", "ox", "xx"):
             scratch[name + "_" + side] = (inputs[weight].shape, BF16)
-    copies = 64 + chunks * (5 + 2 * (peers - 1)) + peers
+    copies = 96 + chunks * (5 + 2 * (peers - 1)) + peers
     names = list(inputs) + list(outputs) + list(scratch) + ["sems"]
     results = pl.pallas_call(
         functools.partial(block_kernel, n, size, names),
@@ -620,13 +667,29 @@
             collective_id=0, has_side_effects=True, vmem_limit_bytes=LIMIT
         ),
     )(*inputs.values())
-    got = dict(zip(outputs, results))
-    return (
-        got["out_b"], got["out_x"], got["o_gain1"][0], got["o_shift1"][0],
-        got["out_q"].reshape(half, 3, width), got["o_bias_q"][0], got["o_bias_v"][0],
-        got["o_table"], got["out_p"], got["o_bias_p"][0], got["o_gain2"][0], got["o_shift2"][0],
-        got["out_e"], got["o_bias_e"][0], got["out_r"], got["o_bias_r"][0],
-    )
+    line, big = pl.BlockSpec(memory_space=pltpu.VMEM), pl.BlockSpec(memory_space=pl.ANY)
+    vec = jax.ShapeDtypeStruct((1, half), F32)
+    tokens = block_input.shape
+    held = [(half, hid), (hid, half), tokens, (3, half, width), (width, half)]
+    shape = jax.ShapeDtypeStruct
+    final = pl.pallas_call(
+        functools.partial(deliver_kernel, slices),
+        name="deliver",
+        out_shape=(
+            shape(tokens, BF16), shape(tokens, F32), vec, vec, shape(held[3], F32), vec, vec,
+            shape((heads, entries), F32), shape(held[4], F32), vec, vec, vec,
+            shape(held[0], F32), shape((1, hid), F32), shape(held[1], F32), vec,
+        ),
+        in_specs=[VMEM] * 4,
+        out_specs=(big, big, line, line, big, line, line, line, big, line, line, line, big, line, big, line),
+        scratch_shapes=[pltpu.VMEM(h, F32) for h in held] + [pltpu.SemaphoreType.DMA((6,))],
+    )(*results)
+    final = list(final)
+    for at in (2, 3, 5, 6, 9, 10, 11, 13, 15):
+        final[at] = final[at][0]
+    final[4] = final[4].transpose(1, 0, 2)
+    final[7] = final[7].T
+    return tuple(final)
 
 
 def solution(mesh):

time: 150 us -> 114 us (0.76)
  Pallas kernels: 131 us -> 112 us
  local copies, waits for them, and re-layouts: 18.3 us -> 1.36 us
    pallas_call x1, Pallas kernels: 131 us -> 107 us  [per_device(): pl.pallas_call(functools.partial(block_kernel, n, size, names), name='blo...]
    unnamed x48 -> x0, local copies, waits for them, and re-layouts: 14.5 us -> none
    pallas_call x0 -> x1, Pallas kernels: none -> 4.34 us  [per_device(): pl.pallas_call(functools.partial(deliver_kernel, slices), name='deliver',...]
    reshape x2 -> x0, local copies, waits for them, and re-layouts: 1.6 us -> none  [the longest x1 0.92 us: per_device(): qkv_weight.reshape(half, 3 * width)]
where the time goes in v1:
time: 114 us
  Pallas kernels  112 us (98%)
  local copies, waits for them, and re-layouts  1.36 us (1%)
    pallas_call x1, Pallas kernels, per_device(): pl.pallas_call(functools.partial(block_kernel, n, size, names), name='blo...  107 us
    pallas_call x1, Pallas kernels, per_device(): pl.pallas_call(functools.partial(deliver_kernel, slices), name='deliver',...  4.34 us

profile of v1, /device:TPU:0, one launch (start us, length us, event | category | flops | bytes accessed | tf_op | source)
XLA Modules:
  0.0 113.9 jit_solution(7904218557275478141)
XLA Ops:
  0.6 1.4 %pad.4.refs_12_ = s32[49,128]{1,0:T(8,128)} pad(s32[49,49]{1,0:T(8,128)} %param.25, s32[]{:T(128)} %constant.0.clone.1), padding=0_0x0_79 | pad | bytes 34696 | tf_op jit(solution)/shard_map/jit(_pad)/pad | solution.py:611
  2.0 107.4 %block.1 = (bf16[3072,256]{1,0:T(8,128)(2,1)}, bf16[784,256]{1,0:T(8,128)(2,1)}, bf16[784,256]{1,0:T(8,128)(2,1)}, f32[24,256]{1,0:T(8,128)}) custom-call(bf16[784,256]{1,0:T(8,128)(2,1)} %refs_0_.1, bf16[784,256]{1,0:T(8,128)(2,1)} %refs_1_.1, f32[1,256]{1,0:T(1,128)} %bitcast.25, f32[1,256]{1,0:T(1,128)} %bitcast.26, f32[1,256]{1,0:T(1,128)} %bitcast.27, ...), custom_call_target="tpu_custom_call" | custom-call | tf_op jit(solution)/shard_map/block/pallas_call | solution.py:658
  109.4 4.3 %deliver.1 = (bf16[784,256]{1,0:T(8,128)(2,1)}, f32[784,256]{1,0:T(8,128)}, f32[1,256]{1,0:T(1,128)}, f32[1,256]{1,0:T(1,128)}, f32[3,256,256]{2,1,0:T(8,128)}, ...) custom-call(bf16[3072,256]{1,0:T(8,128)(2,1)} %get-tuple-element.36., ...), custom_call_target="tpu_custom_call" | custom-call | tf_op jit(solution)/shard_map/deliver/pallas_call | solution.py:675

commit v2 on v1

--- a/solution.py
+++ b/solution.py
@@ -119,6 +119,13 @@
     for device in [over_col, over_row, pair] + [peer_of(k)[1] for k in range(1, peers)]:
         pl.semaphore_signal(barrier, inc=1, device_id=device, device_id_type=MESH)
 
+    loads = {
+        name: pltpu.make_async_copy(getattr(r, "in_" + name), getattr(r, name), r.loads.at[k])
+        for k, name in enumerate(at[3:] for at in names if at.startswith("in_"))
+    }
+    for copy in loads.values():
+        copy.start()
+
     def start(key, src, dst, device):
         index = len(live)
         live[key] = pltpu.make_async_remote_copy(
@@ -132,6 +139,8 @@
     def tokens_of(image):
         return pl.ds(pl.multiple_of(image * TOK, 16), TOK)
 
+    for copy in loads.values():
+        copy.wait()
     r.vec_own[...] = jnp.zeros_like(r.vec_own)
     r.cvec_own[...] = jnp.zeros_like(r.cvec_own)
     for k, ref in enumerate((r.gain1, r.shift1, r.bias_p, r.gain2, r.shift2, r.bias_r)):
@@ -227,9 +236,10 @@
     fetch("r")
     r.g_away[...] = dot(sel_theirs, r.g_in[...]).astype(BF16)
     start(("g",), r.g_away, r.g_oth, over_row)
-    which = lax.broadcasted_iota(jnp.int32, (entries, LANES), 0)
+    which = lax.broadcasted_iota(jnp.int32, (entries, WINDOW), 0)
+    r.hot[...] = jnp.zeros_like(r.hot)
     for k in range(WINDOW):
-        r.hot[:, k * LANES:(k + 1) * LANES] = jnp.where(which == r.index[k:k + 1], 1.0, 0.0).astype(BF16)
+        r.hot[:, k * LANES:k * LANES + WINDOW] = jnp.where(which == r.index[k:k + 1], 1.0, 0.0).astype(BF16)
     relay_one("q")
     spread = unthird(dot(thirds(r.table[...]), r.hot[...]))
     lane = lax.broadcasted_iota(jnp.int32, (heads, PAD), 1)
@@ -252,6 +262,7 @@
     r.n_one[...] = normed
     r.ln_one[...] = (normed * rvec[0:1] + rvec[1:2]).astype(BF16)
     relay_one("p")
+    relay_one("e")
     relay_three("q")
     relay_two("p")
     arrived("cvec")
@@ -264,8 +275,7 @@
     for b in range(2):
         cols = slice(b * width, (b + 1) * width)
         if b == 1:
-            relay_three("p")
-            relay_one("e")
+            relay_one("r")
             ready("q")
             arrived("bias")
         for s, out in enumerate((r.q, r.k, r.v)):
@@ -283,8 +293,8 @@
             probs = softmax(scores)
             r.probs[b * 4 + w] = probs
             r.mixed[rows, cols] = fold_heads(dot(probs.astype(BF16), r.v[rows, cols]), mask).astype(BF16)
+    relay_three("p")
     relay_two("e")
-    relay_one("r")
     ready("p")
     parts = [
         dot(r.mixed[:, :width], p_side[a][0][...]) + dot(r.mixed[:, width:], p_side[a][1][...])
@@ -294,8 +304,8 @@
     r.middle[...] = middle
     normed_two, inverse_two = norm(middle)
     r.ln_two[...] = (normed_two * rvec[3:4] + rvec[4:5]).astype(BF16)
+    relay_two("r")
     relay_three("e")
-    relay_two("r")
     arrived("g")
     grad = dot(r.perm[...], jnp.concatenate([grad_own, r.g_oth[...]], axis=1))
     r.grad[...] = grad.astype(BF16)
@@ -406,8 +416,10 @@
                 out[down] = t_dot(hidden, r.grad[:, side]).astype(out.dtype)
             if b == 1:
                 away_done(2 * q + 2)
-        home_done(2 * q + 2)
-    advance(6.5)
+                home_done(2 * q)
+        if q in (0, slices - 1):
+            home_done(2 * q + 2)
+    advance(9)
     second = jnp.concatenate(
         [
             dot_t(r.pg[:, :hid], e_side[a][0][...]) + dot_t(r.pg[:, hid:], e_side[a][1][...])
@@ -457,7 +469,7 @@
     ]
     home_done(2 * slices + 1)
     spread_out(0, r.middle[...] + jnp.concatenate(parts, axis=1) + rvec[5:6], r.t_blk)
-    advance(9)
+    advance(12)
 
     for b in (1, 0):
         cols = slice(b * width, (b + 1) * width)
@@ -493,7 +505,7 @@
                 away_done(2 * slices + 2 + s)
             else:
                 home_done(2 * slices + 2 + s)
-        advance(12 if b == 1 else 15)
+        advance(16 if b == 1 else 20)
     first = jnp.concatenate(
         [
             sum(
@@ -521,13 +533,13 @@
     start(("s0",), r.small.at[0:32], r.s_col, over_col)
     in_grad = r.mgrad[...] + norm_backward(first, rvec[0:1], r.n_one[...], inverse_one)
     spread_out(1, in_grad, r.t_in)
-    advance(18)
+    advance(24)
     pass_on(0, r.t_blk)
     arrived("s0")
     r.s_mid[0:8] = r.small[8:16] + r.s_col[8:16]
     r.s_mid[8:24] = r.small[32:48] + r.s_col[16:32]
     start(("s1",), r.s_mid, r.s_row, over_row)
-    advance(22)
+    advance(30)
     collect(0, r.t_blk, r.out_b)
     late = 2.6 + drain * chunks
     advance(late)
@@ -608,13 +620,12 @@
     rows = 2 * hid + 4 * half
     size = max(n * 16, half)
     chunks, peers, wide = rows // size, n // 2, size // 2
-    index = jnp.pad(position_index, ((0, 0), (0, LANES - WINDOW)), constant_values=-1)
     inputs = dict(
         x_in=block_input, g_in=out_grad,
         gain1=first_gain[None], shift1=first_shift[None], bias_p=proj_bias[None],
         gain2=second_gain[None], shift2=second_shift[None], bias_r=reduce_bias[None],
         bias_q=query_bias[None], bias_v=value_bias[None], bias_e=expand_bias[None],
-        table=position_table.T, index=index,
+        table=position_table.T, index=position_index,
         wq=qkv_weight.transpose(1, 0, 2), wp=proj_weight, we=expand_weight, wr=reduce_weight,
     )
     outputs = dict(
@@ -654,15 +665,17 @@
         for side in ("xo", "ox", "xx"):
             scratch[name + "_" + side] = (inputs[weight].shape, BF16)
     copies = 96 + chunks * (5 + 2 * (peers - 1)) + peers
-    names = list(inputs) + list(outputs) + list(scratch) + ["sems"]
+    for name, value in inputs.items():
+        scratch[name] = (value.shape, value.dtype)
+    names = ["in_" + name for name in inputs] + list(outputs) + list(scratch) + ["loads", "sems"]
     results = pl.pallas_call(
         functools.partial(block_kernel, n, size, names),
         name="block",
         out_shape=tuple(jax.ShapeDtypeStruct(*out) for out in outputs.values()),
-        in_specs=[VMEM] * len(inputs),
+        in_specs=[pl.BlockSpec(memory_space=pltpu.HBM)] * len(inputs),
         out_specs=tuple([VMEM] * len(outputs)),
         scratch_shapes=[pltpu.VMEM(*shape) for shape in scratch.values()]
-        + [pltpu.SemaphoreType.DMA((2, copies))],
+        + [pltpu.SemaphoreType.DMA((len(inputs),)), pltpu.SemaphoreType.DMA((2, copies))],
         compiler_params=pltpu.CompilerParams(
             collective_id=0, has_side_effects=True, vmem_limit_bytes=LIMIT
         ),

time: 114 us -> 100 us (0.88)
  Pallas kernels: 112 us -> 99 us
  local copies, waits for them, and re-layouts: 1.36 us -> 0 us
    pallas_call x1, Pallas kernels: 107 us -> 94.7 us  [per_device(): pl.pallas_call(functools.partial(block_kernel, n, size, names), name='blo...]
    pad x1 -> x0, local copies, waits for them, and re-layouts: 1.36 us -> none  [per_device(): jnp.pad(position_index, ((0, 0), (0, LANES - WINDOW)), constant_values=-1)]
where the time goes in v2:
time: 100 us; the launch traced here: 99.8 us
  Pallas kernels  99 us (99%)
    pallas_call x1, Pallas kernels, per_device(): pl.pallas_call(functools.partial(block_kernel, n, size, names), name='blo...  94.7 us
    pallas_call x1, Pallas kernels, per_device(): pl.pallas_call(functools.partial(deliver_kernel, slices), name='deliver',...  4.34 us

profile of v2, /device:TPU:0, one launch (start us, length us, event | category | flops | bytes accessed | tf_op | source)
XLA Modules:
  0.0 99.8 jit_solution(16795101525916863208)
XLA Ops:
  0.7 94.7 %block.1 = (bf16[3072,256]{1,0:T(8,128)(2,1)}, bf16[784,256]{1,0:T(8,128)(2,1)}, bf16[784,256]{1,0:T(8,128)(2,1)}, f32[24,256]{1,0:T(8,128)}) custom-call(bf16[784,256]{1,0:T(8,128)(2,1)} %refs_0_.1, bf16[784,256]{1,0:T(8,128)(2,1)} %refs_1_.1, f32[1,256]{1,0:T(1,128)} %bitcast.25, f32[1,256]{1,0:T(1,128)} %bitcast.26, f32[1,256]{1,0:T(1,128)} %bitcast.27, ...), custom_call_target="tpu_custom_call" | custom-call | tf_op jit(solution)/shard_map/block/pallas_call | solution.py:671
  95.3 4.3 %deliver.1 = (bf16[784,256]{1,0:T(8,128)(2,1)}, f32[784,256]{1,0:T(8,128)}, f32[1,256]{1,0:T(1,128)}, f32[1,256]{1,0:T(1,128)}, f32[3,256,256]{2,1,0:T(8,128)}, ...) custom-call(bf16[3072,256]{1,0:T(8,128)(2,1)} %get-tuple-element.36., ...), custom_call_target="tpu_custom_call" | custom-call | tf_op jit(solution)/shard_map/deliver/pallas_call | solution.py:688
